TPU v7x, 128 devices: a whole 4x4x4 slice. The times are simulated.
128 devices in a mesh: leaf: 8 (over x, core), front: 16 (over z, y).
Axes of the slice: x: 4, y: 4, z: 4, core: 2. Of those that a mesh axis runs over, the one named last changes fastest.
Arguments:
- front_matrix: float32 [8, 2048, 2048], P('leaf', 'front'), as said below
- child_blocks: float32 [128, 8, 3, 128, 128], P(('leaf', 'front')), may hold values from -0.046875 to 0.046875
- child_target: int32 [128, 8, 3], P(('leaf', 'front')), may hold values from 0 to 15, as said below
- child_count: int32 [128, 8], P(('leaf', 'front')), may hold values from 1 to 3, as said below
- shot_rhs: float32 [8, 64, 2048], P('leaf'), may hold values from -6 to 6
Outputs:
- factored: float32 [8, 2048, 2048], P('leaf', 'front')
- eliminated: float32 [8, 64, 2048], P('leaf')
Inputs may be any that keep to these rules, and one draw needn't show every extreme that they name: `child_target`: A bucket's code places its block on a row block that the receiving device (leaf index of the bucket, front index of the sender) holds, at a column block no later than that row block. Slots from child_count on are empty and hold no data. In every draw some leaf index receives 3 live blocks from every sender. `front_matrix`: after the child blocks are added, the symmetric matrix that each front's lower triangle defines is positive definite.
All inputs are finite; a program needn't handle non-finite values.
Results may differ from a plain program's by a relative error of at most 0.00013.
Values sent between devices are 32-bit elements; how exact they have to be, the bound alone decides.
No kernel may reach another device: no remote copies, remote signals or barrier semaphores. Data moves between devices by JAX's collectives and lax.ppermute only.
A program may use at most 64 MiB of HBM per device.

v0:
```python
import jax
import jax.numpy as jnp
from jax import lax
from jax.sharding import PartitionSpec as P

BLOCK = 128
PIVOTS = 1024


def spread(value, axis, source):
    kept = jnp.where(lax.axis_index(axis) == source, value, 0).astype(value.dtype)
    return lax.psum(kept, axis)


def lower_sym(square):
    return jnp.tril(square) + jnp.swapaxes(jnp.tril(square, -1), -1, -2)


def right_solve(factor, values):
    solved = jax.scipy.linalg.solve_triangular(factor, jnp.swapaxes(values, 1, 2), lower=True)
    return jnp.swapaxes(solved, 1, 2)


def local(front_matrix, child_blocks, child_target, child_count, shot_rhs):
    fronts_here, rows_local, order_here = front_matrix.shape
    leaf_count = lax.axis_size("leaf")
    capacity = child_blocks.shape[2]
    slot_ids = lax.broadcasted_iota(jnp.int32, child_target.shape, 2)
    live_code = jnp.where(slot_ids < child_count[:, :, None], child_target, -1)
    arrived, codes = (
        lax.all_to_all(child_blocks, "leaf", split_axis=1, concat_axis=1, tiled=True),
        lax.all_to_all(live_code, "leaf", split_axis=1, concat_axis=1, tiled=True),
    )
    count_in = leaf_count * capacity
    flat_blocks = arrived.reshape(count_in, BLOCK * BLOCK)
    flat_codes = codes.reshape(count_in)
    block_cols = order_here // BLOCK
    block_rows = rows_local // BLOCK
    slot_total = fronts_here * block_rows * block_cols
    one_hot = (
        lax.broadcasted_iota(jnp.int32, (slot_total, count_in), 0) == flat_codes[None, :]
    ).astype(jnp.float32)
    summed = jnp.dot(
        one_hot, flat_blocks, precision=lax.Precision.HIGHEST, preferred_element_type=jnp.float32
    )
    extended = summed.reshape(fronts_here, block_rows, block_cols, BLOCK, BLOCK)
    extended = extended.transpose(0, 1, 3, 2, 4).reshape(fronts_here, rows_local, order_here)
    matrix = front_matrix + extended
    my_index = lax.axis_index("front")
    row_global = my_index * rows_local + lax.broadcasted_iota(jnp.int32, (rows_local, 1), 0)
    current_rhs = shot_rhs
    left_parts = []
    diag_parts = []
    solved_parts = []
    for pivot_step in range(PIVOTS // BLOCK):
        start_col = pivot_step * BLOCK
        end_col = start_col + BLOCK
        column_panel = matrix[:, :, start_col:end_col]
        owner_index = start_col // rows_local
        owner_offset = start_col - owner_index * rows_local
        identity_mat = jnp.broadcast_to(jnp.eye(BLOCK, dtype=jnp.float32), column_panel.shape)
        safe_square = jnp.where(my_index == owner_index, lower_sym(column_panel), identity_mat)
        own_factor = jnp.linalg.cholesky(safe_square)
        pivot_factor = spread(own_factor, "front", owner_index)
        my_panel = right_solve(pivot_factor, column_panel)
        my_panel = jnp.where(row_global < start_col, jnp.float32(0.0), my_panel)
        placed = jnp.where(my_index == owner_index, pivot_factor, my_panel)
        my_panel = my_panel.at[:, owner_offset : owner_offset + BLOCK].set(placed)
        full_panel = lax.all_gather(my_panel, "front", axis=1, tiled=True)
        tail_panel = full_panel[:, end_col:]
        update = jnp.einsum(
            "frb,fcb->frc",
            my_panel,
            tail_panel,
            precision=lax.Precision.HIGHEST,
            preferred_element_type=jnp.float32,
        )
        matrix = matrix.at[:, :, end_col:].add(-update)
        zeta = right_solve(pivot_factor, current_rhs[:, :, start_col:end_col])
        rhs_update = jnp.einsum(
            "fnb,fcb->fnc",
            zeta,
            tail_panel,
            precision=lax.Precision.HIGHEST,
            preferred_element_type=jnp.float32,
        )
        current_rhs = current_rhs.at[:, :, end_col:].add(-rhs_update)
        pivots_now = jnp.diagonal(pivot_factor, axis1=1, axis2=2)
        left_parts.append(my_panel / pivots_now[:, None, :])
        diag_parts.append(pivots_now * pivots_now)
        solved_parts.append(zeta * pivots_now[:, None, :])
    col_global = lax.broadcasted_iota(jnp.int32, (1, order_here), 1)
    combined = jnp.concatenate(left_parts + [matrix[:, :, PIVOTS:]], axis=2)
    combined = jnp.where(row_global < col_global, jnp.float32(0.0), combined)
    diag_full = jnp.concatenate(
        diag_parts + [jnp.zeros((fronts_here, order_here - PIVOTS), jnp.float32)], axis=1
    )
    on_diagonal = (row_global == col_global) & (col_global < PIVOTS)
    factored = jnp.where(on_diagonal, diag_full[:, None, :], combined)
    eliminated = jnp.concatenate(solved_parts + [current_rhs[:, :, PIVOTS:]], axis=2)
    return (factored, eliminated)


def solution(mesh):
    return jax.shard_map(
        local,
        mesh=mesh,
        in_specs=(
            P("leaf", "front", None),
            P(("leaf", "front"), None, None, None, None),
            P(("leaf", "front"), None, None),
            P(("leaf", "front"), None),
            P("leaf", None, None),
        ),
        out_specs=(P("leaf", "front", None), P("leaf", None, None)),
        check_vma=False,
    )
```

profile of v0, /device:TPU:0, one launch (start us, length us, event | category | flops | bytes accessed | tf_op | source)
XLA Modules:
  0.0 1286.4 jit_solution(12583845993747838078)
XLA Ops:
  8.6 9.4 all_to_all.10
  18.1 3.6 all-to-all-start.1
  24.9 18.3 %all-to-all-done.1 = f32[1,8,3,128,128]{4,3,2,0,1:T(8,128)S(1)} async-done(((f32[1,8,3,128,128]{4,3,2,0,1:T(8,128)}), f32[1,8,3,128,128]{4,3,2,0,1:T(8,128)S(1)}, u32[]{:S(2)}, u32[]{:S(2)}) %all-to-all-start.1) | async-done | bytes 1572896 | tf_op jit(solution)/shard_map/all_to_all | solution.py:31
  43.2 2.6 fusion.31
  45.8 2.6 copy.268
  50.1 11.7 custom-call.46
  63.9 81.6 %all-reduce.9.cloned.1.call-done = f32[1,128,128]{2,1,0:T(8,128)} async-done(((f32[1,128,128]{2,1,0:T(8,128)}), f32[1,128,128]{2,1,0:T(8,128)}) %all-reduce.9.cloned.1.call-update) | async-done | bytes 65552 | tf_op jit(solution)/shard_map/psum | solution.py:12
  146.3 9.8 custom-call.47
  160.2 41.1 %all-gather.9.cloned.1.call-done = f32[1,2048,128]{2,1,0:T(8,128)} async-done(((f32[1,128,128]{2,1,0:T(8,128)}), f32[1,2048,128]{2,1,0:T(8,128)}) %all-gather.9.cloned.1.call-update) | async-done | bytes 1048592 | tf_op jit(solution)/shard_map/all_gather | solution.py:69
  201.3 2.2 fusion.13
  203.9 11.7 custom-call.48
  217.7 80.3 %all-reduce.11.cloned.1.call-done = f32[1,128,128]{2,1,0:T(8,128)} async-done(((f32[1,128,128]{2,1,0:T(8,128)}), f32[1,128,128]{2,1,0:T(8,128)}) %all-reduce.11.cloned.1.call-update) | async-done | bytes 65552 | tf_op jit(solution)/shard_map/psum | solution.py:12
  298.8 9.8 custom-call.49
  312.1 41.7 %all-gather.11.cloned.1.call-done = f32[1,2048,128]{2,1,0:T(8,128)} async-done(((f32[1,128,128]{2,1,0:T(8,128)}), f32[1,2048,128]{2,1,0:T(8,128)}) %all-gather.11.cloned.1.call-update) | async-done | bytes 1048592 | tf_op jit(solution)/shard_map/all_gather | solution.py:69
  353.8 2.1 fusion.12
  356.3 11.7 custom-call.50
  370.1 80.3 %all-reduce.13.cloned.1.call-done = f32[1,128,128]{2,1,0:T(8,128)} async-done(((f32[1,128,128]{2,1,0:T(8,128)}), f32[1,128,128]{2,1,0:T(8,128)}) %all-reduce.13.cloned.1.call-update) | async-done | bytes 65552 | tf_op jit(solution)/shard_map/psum | solution.py:12
  451.2 9.8 custom-call.51
  461.1 2.0 gather_fusion.2
  465.9 40.3 %all-gather.13.cloned.1.call-done = f32[1,2048,128]{2,1,0:T(8,128)} async-done(((f32[1,128,128]{2,1,0:T(8,128)}), f32[1,2048,128]{2,1,0:T(8,128)}) %all-gather.13.cloned.1.call-update) | async-done | bytes 1048592 | tf_op jit(solution)/shard_map/all_gather | solution.py:69
  506.3 2.0 fusion.11
  508.6 11.7 custom-call.52
  523.3 79.7 %all-reduce.15.cloned.1.call-done = f32[1,128,128]{1,2,0:T(8,128)} async-done(((f32[1,128,128]{1,2,0:T(8,128)}), f32[1,128,128]{1,2,0:T(8,128)}) %all-reduce.15.cloned.1.call-update) | async-done | bytes 65552 | tf_op jit(solution)/shard_map/psum | solution.py:12
  603.9 9.8 custom-call.53
  613.7 2.0 gather_fusion.3
  617.3 42.3 %all-gather.15.cloned.1.call-done = f32[1,2048,128]{1,2,0:T(8,128)} async-done(((f32[1,128,128]{1,2,0:T(8,128)}), f32[1,2048,128]{1,2,0:T(8,128)}) %all-gather.15.cloned.1.call-update) | async-done | bytes 1048592 | tf_op jit(solution)/shard_map/all_gather | solution.py:69
  659.6 2.0 fusion.7
  661.9 11.7 custom-call.54
  675.9 80.3 %all-reduce.17.cloned.1.call-done = f32[1,128,128]{1,2,0:T(8,128)} async-done(((f32[1,128,128]{1,2,0:T(8,128)}), f32[1,128,128]{1,2,0:T(8,128)}) %all-reduce.17.cloned.1.call-update) | async-done | bytes 65552 | tf_op jit(solution)/shard_map/psum | solution.py:12
  757.1 9.8 custom-call.55
  766.9 2.0 gather_fusion.4
  770.2 42.6 %all-gather.17.cloned.1.call-done = f32[1,2048,128]{1,2,0:T(8,128)} async-done(((f32[1,128,128]{1,2,0:T(8,128)}), f32[1,2048,128]{1,2,0:T(8,128)}) %all-gather.17.cloned.1.call-update) | async-done | bytes 1048592 | tf_op jit(solution)/shard_map/all_gather | solution.py:69
  815.1 11.7 custom-call.56
  829.0 80.3 %all-reduce.19.cloned.1.call-done = f32[1,128,128]{1,2,0:T(8,128)} async-done(((f32[1,128,128]{1,2,0:T(8,128)}), f32[1,128,128]{1,2,0:T(8,128)}) %all-reduce.19.cloned.1.call-update) | async-done | bytes 65552 | tf_op jit(solution)/shard_map/psum | solution.py:12
  910.2 9.8 custom-call.57
  920.1 2.0 gather_fusion.5
  928.8 37.1 %all-gather.19.cloned.1.call-done = f32[1,2048,128]{1,2,0:T(8,128)} async-done(((f32[1,128,128]{1,2,0:T(8,128)}), f32[1,2048,128]{1,2,0:T(8,128)}) %all-gather.19.cloned.1.call-update) | async-done | bytes 1048592 | tf_op jit(solution)/shard_map/all_gather | solution.py:69
  968.1 11.7 custom-call.58
  982.0 80.3 %all-reduce.21.cloned.1.call-done = f32[1,128,128]{1,2,0:T(8,128)} async-done(((f32[1,128,128]{1,2,0:T(8,128)}), f32[1,128,128]{1,2,0:T(8,128)}) %all-reduce.21.cloned.1.call-update) | async-done | bytes 65552 | tf_op jit(solution)/shard_map/psum | solution.py:12
  1063.3 9.8 custom-call.59
  1073.1 2.0 gather_fusion.6
  1082.5 37.1 %all-gather.21.cloned.1.call-done = f32[1,2048,128]{1,2,0:T(8,128)} async-done(((f32[1,128,128]{1,2,0:T(8,128)}), f32[1,2048,128]{1,2,0:T(8,128)}) %all-gather.21.cloned.1.call-update) | async-done | bytes 1048592 | tf_op jit(solution)/shard_map/all_gather | solution.py:69
  1119.6 2.2 fusion.1
  1122.2 11.7 custom-call.60
  1138.0 78.5 %all-reduce.23.cloned.1.call-done = f32[1,128,128]{2,1,0:T(8,128)} async-done(((f32[1,128,128]{2,1,0:T(8,128)}), f32[1,128,128]{2,1,0:T(8,128)}) %all-reduce.23.cloned.1.call-update) | async-done | bytes 65552 | tf_op jit(solution)/shard_map/psum | solution.py:12
  1217.4 9.8 custom-call.61
  1234.3 38.1 %all-gather.23.cloned.1.call-done = f32[1,2048,128]{2,1,0:T(8,128)} async-done(((f32[1,128,128]{2,1,0:T(8,128)}), f32[1,2048,128]{2,1,0:T(8,128)}) %all-gather.23.cloned.1.call-update) | async-done | bytes 1048592 | tf_op jit(solution)/shard_map/all_gather | solution.py:69
  1272.4 2.4 fusion.36
  (260 shorter events, 77.9 us)
Async XLA Ops:
  18.1 25.1 %all-to-all-start.1 = ((f32[1,8,3,128,128]{4,3,2,0,1:T(8,128)}), f32[1,8,3,128,128]{4,3,2,0,1:T(8,128)S(1)}, u32[]{:S(2)}, u32[]{:S(2)}) async-start(f32[1,8,3,128,128]{4,3,2,0,1:T(8,128)} %bitcast.595), calls=%async_computation.1 | async-start | bytes 3145728 | tf_op jit(solution)/shard_map/all_to_all | solution.py:31
  21.7 123.8 %all-reduce.9.cloned.1.call-start = ((), (), s32[]{:S(2)}) async-start(), calls=%async_computation.2 | async-start | bytes 131072 | tf_op jit(solution)/shard_map/psum | solution.py:12
  63.8 137.5 %all-gather.9.cloned.1.call-start = ((), (), s32[]{:S(2)}) async-start(), calls=%async_computation.3 | async-start | bytes 1114112 | tf_op jit(solution)/shard_map/all_gather | solution.py:69
  159.9 138.1 %all-reduce.11.cloned.1.call-start = ((), (), s32[]{:S(2)}) async-start(), calls=%async_computation.4 | async-start | bytes 131072 | tf_op jit(solution)/shard_map/psum | solution.py:12
  217.6 136.2 %all-gather.11.cloned.1.call-start = ((), (), s32[]{:S(2)}) async-start(), calls=%async_computation.5 | async-start | bytes 1114112 | tf_op jit(solution)/shard_map/all_gather | solution.py:69
  311.5 138.8 %all-reduce.13.cloned.1.call-start = ((), (), s32[]{:S(2)}) async-start(), calls=%async_computation.6 | async-start | bytes 131072 | tf_op jit(solution)/shard_map/psum | solution.py:12
  370.0 136.2 %all-gather.13.cloned.1.call-start = ((), (), s32[]{:S(2)}) async-start(), calls=%async_computation.7 | async-start | bytes 1114112 | tf_op jit(solution)/shard_map/all_gather | solution.py:69
  461.0 47.3 %copy-start.16 = (f32[1,128,128]{1,2,0:T(8,128)}, f32[1,128,128]{1,2,0:T(8,128)S(1)}, u32[]{:S(2)}) copy-start(f32[1,128,128]{1,2,0:T(8,128)S(1)} %custom-call.51) | copy-start | bytes 196612
  464.0 139.0 %all-reduce.15.cloned.1.call-start = ((), (), s32[]{:S(2)}) async-start(), calls=%async_computation.8 | async-start | bytes 131072 | tf_op jit(solution)/shard_map/psum | solution.py:12
  522.6 137.0 %all-gather.15.cloned.1.call-start = ((), (), s32[]{:S(2)}) async-start(), calls=%async_computation.9 | async-start | bytes 1114112 | tf_op jit(solution)/shard_map/all_gather | solution.py:69
  613.7 3.6 copy-start.18
  616.7 139.5 %all-reduce.17.cloned.1.call-start = ((), (), s32[]{:S(2)}) async-start(), calls=%async_computation.10 | async-start | bytes 131072 | tf_op jit(solution)/shard_map/psum | solution.py:12
  616.9 42.6 %copy-start.14 = (f32[1,128,128]{1,2,0:T(8,128)S(1)}, f32[1,128,128]{1,2,0:T(8,128)}, u32[]{:S(2)}) copy-start(f32[1,128,128]{1,2,0:T(8,128)} %get-tuple-element.372) | copy-start | bytes 196612
  675.8 137.0 %all-gather.17.cloned.1.call-start = ((), (), s32[]{:S(2)}) async-start(), calls=%async_computation.11 | async-start | bytes 1114112 | tf_op jit(solution)/shard_map/all_gather | solution.py:69
  766.9 47.8 %copy-start.22 = (f32[1,128,128]{1,2,0:T(8,128)}, f32[1,128,128]{1,2,0:T(8,128)S(1)}, u32[]{:S(2)}) copy-start(f32[1,128,128]{1,2,0:T(8,128)S(1)} %custom-call.55) | copy-start | bytes 196612
  769.9 139.4 %all-reduce.19.cloned.1.call-start = ((), (), s32[]{:S(2)}) async-start(), calls=%async_computation.12 | async-start | bytes 131072 | tf_op jit(solution)/shard_map/psum | solution.py:12
  814.7 110.4 %copy-start.15 = (f32[1,64,2048]{2,1,0:T(8,128)S(1)}, f32[1,64,2048]{2,1,0:T(8,128)}, u32[]{:S(2)}) copy-start(f32[1,64,2048]{2,1,0:T(8,128)} %param.78) | copy-start | bytes 1572868
  814.7 111.2 %copy-start = (f32[1,2048,128]{2,1,0:T(8,128)S(1)}, f32[1,2048,128]{2,1,0:T(8,128)}, u32[]{:S(2)}) copy-start(f32[1,2048,128]{2,1,0:T(8,128)} %all-gather.9.cloned.1.call-done) | copy-start | bytes 3145732
  828.9 137.0 %all-gather.19.cloned.1.call-start = ((), (), s32[]{:S(2)}) async-start(), calls=%async_computation.13 | async-start | bytes 1114112 | tf_op jit(solution)/shard_map/all_gather | solution.py:69
  920.0 7.1 copy-start.20
  923.0 42.9 %copy-start.13 = (f32[1,128,128]{1,2,0:T(8,128)S(1)}, f32[1,128,128]{1,2,0:T(8,128)}, u32[]{:S(2)}) copy-start(f32[1,128,128]{1,2,0:T(8,128)} %get-tuple-element.376) | copy-start | bytes 196612
  923.0 139.3 %all-reduce.21.cloned.1.call-start = ((), (), s32[]{:S(2)}) async-start(), calls=%async_computation.14 | async-start | bytes 131072 | tf_op jit(solution)/shard_map/psum | solution.py:12
  967.7 109.2 %copy-start.1 = (f32[1,2048,128]{2,1,0:T(8,128)S(1)}, f32[1,2048,128]{2,1,0:T(8,128)}, u32[]{:S(2)}) copy-start(f32[1,2048,128]{2,1,0:T(8,128)} %all-gather.11.cloned.1.call-done) | copy-start | bytes 3145732
  967.7 109.2 %copy-start.6 = (f32[1,64,1920]{2,1,0:T(8,128)S(1)}, f32[1,64,1920]{2,1,0:T(8,128)}, u32[]{:S(2)}) copy-start(f32[1,64,1920]{2,1,0:T(8,128)} %copy-done.5) | copy-start | bytes 1474564
  982.0 96.1 %copy-start.17 = (f32[1,128,128]{1,2,0:T(8,128)S(1)}, f32[1,128,128]{1,2,0:T(8,128)}, u32[]{:S(2)}) copy-start(f32[1,128,128]{1,2,0:T(8,128)} %copy-done.16) | copy-start | bytes 196612
  982.0 137.6 %all-gather.21.cloned.1.call-start = ((), (), s32[]{:S(2)}) async-start(), calls=%async_computation.15 | async-start | bytes 1114112 | tf_op jit(solution)/shard_map/all_gather | solution.py:69
  1063.2 15.7 %copy-start.2 = (f32[1,2048,128]{2,1,0:T(8,128)S(1)}, f32[1,2048,128]{2,1,0:T(8,128)}, u32[]{:S(2)}) copy-start(f32[1,2048,128]{2,1,0:T(8,128)} %all-gather.13.cloned.1.call-done) | copy-start | bytes 3145732
  1073.1 3.8 copy-start.24
  1075.1 3.8 copy-start.26
  1076.7 139.9 %all-reduce.23.cloned.1.call-start = ((), (), s32[]{:S(2)}) async-start(), calls=%async_computation.16 | async-start | bytes 131072 | tf_op jit(solution)/shard_map/psum | solution.py:12
  1076.9 3.1 copy-start.19
  1076.9 3.9 copy-start.3
  1078.9 2.5 copy-start.23
  1081.4 0.9 copy-start.8
  1081.4 38.2 %copy-start.11 = (f32[1,128,128]{1,2,0:T(8,128)S(1)}, f32[1,128,128]{1,2,0:T(8,128)}, u32[]{:S(2)}) copy-start(f32[1,128,128]{1,2,0:T(8,128)} %get-tuple-element.378) | copy-start | bytes 196612
  1082.5 54.0 %copy-start.4 = (f32[1,2048,128]{1,2,0:T(8,128)S(1)}, f32[1,2048,128]{1,2,0:T(8,128)}, u32[]{:S(2)}) copy-start(f32[1,2048,128]{1,2,0:T(8,128)} %all-gather.17.cloned.1.call-done) | copy-start | bytes 3145732
  1122.0 107.2 %copy-start.30 = (pred[128]{0:T(512)(128)(4,1)S(1)}, pred[128]{0:T(512)(128)(4,1)}, u32[]{:S(2)}) copy-start(pred[128]{0:T(512)(128)(4,1)} %broadcast_compare_fusion) | copy-start | bytes 388
  1122.1 108.0 %copy-start.21 = (f32[1,128,128]{1,2,0:T(8,128)S(1)}, f32[1,128,128]{1,2,0:T(8,128)}, u32[]{:S(2)}) copy-start(f32[1,128,128]{1,2,0:T(8,128)} %copy-done.20) | copy-start | bytes 196612
  1134.0 97.0 %copy-start.7 = (f32[1,2048,128]{1,2,0:T(8,128)S(1)}, f32[1,2048,128]{1,2,0:T(8,128)}, u32[]{:S(2)}) copy-start(f32[1,2048,128]{1,2,0:T(8,128)} %all-gather.19.cloned.1.call-done) | copy-start | bytes 3145732
  1136.2 136.2 %all-gather.23.cloned.1.call-start = ((), (), s32[]{:S(2)}) async-start(), calls=%async_computation.17 | async-start | bytes 1114112 | tf_op jit(solution)/shard_map/all_gather | solution.py:69
  1138.0 93.4 %copy-start.27 = (f32[128]{0:T(128)S(1)}, f32[128]{0:T(128)}, u32[]{:S(2)}) copy-start(f32[128]{0:T(128)} %copy-done.26) | copy-start | bytes 1540
  1138.0 93.5 %copy-start.25 = (f32[1,128,128]{1,2,0:T(8,128)S(1)}, f32[1,128,128]{1,2,0:T(8,128)}, u32[]{:S(2)}) copy-start(f32[1,128,128]{1,2,0:T(8,128)} %copy-done.24) | copy-start | bytes 196612
  1138.0 94.3 %copy-start.9 = (f32[1,2048,128]{1,2,0:T(8,128)S(1)}, f32[1,2048,128]{1,2,0:T(8,128)}, u32[]{:S(2)}) copy-start(f32[1,2048,128]{1,2,0:T(8,128)} %all-gather.21.cloned.1.call-done) | copy-start | bytes 3145732
  1231.0 41.5 %copy-start.12 = (f32[1,128,128]{2,1,0:T(8,128)S(1)}, f32[1,128,128]{2,1,0:T(8,128)}, u32[]{:S(2)}) copy-start(f32[1,128,128]{2,1,0:T(8,128)} %get-tuple-element.380) | copy-start | bytes 196612
  1232.3 42.6 %copy-start.31 = (s32[128]{0:T(128)S(1)}, s32[128]{0:T(128)}, u32[]{:S(2)}) copy-start(s32[128]{0:T(128)} %iota_add_fusion.1) | copy-start | bytes 1540
  1276.6 1.3 copy-start.10
  1276.6 1.6 copy-start.28
  1278.9 0.8 copy-start.29
  (1 other events, 0.8 us)
Sparse Core Ops, SparseCore 0:
  63.9 81.5 all-reduce.8
  160.0 41.2 all-gather.8
  217.7 80.2 all-reduce.10
  311.7 42.1 all-gather.10
  370.1 80.1 all-reduce.12
  464.1 42.1 all-gather.12
  522.7 80.2 all-reduce.14
  616.8 42.7 all-gather.14
  675.9 80.2 all-reduce.16
  770.0 42.7 all-gather.16
  829.0 80.2 all-reduce.18
  923.1 42.7 all-gather.18
  982.1 80.1 all-reduce.20
  1076.8 42.7 all-gather.20
  1136.3 80.2 all-reduce.22
  1230.3 42.1 all-gather.22
where the time goes:
time: 1300 us; the launch traced here: 1290 us
  waiting for transfers between devices  980 us (75%)
  other arithmetic  202 us (16%)
  matrix products  41.7 us (3%)
  local copies, waits for them, and re-layouts  31.6 us (2%)
  between operations  15.4 us (1%)
    psum x8, waiting for transfers between devices, spread(): return lax.psum(kept, axis)  641 us
    all_gather x8, waiting for transfers between devices, local(): full_panel = lax.all_gather(my_panel, 'front', axis=1, tiled=True)  320 us
    another operation x24, other arithmetic, local(): own_factor = jnp.linalg.cholesky(safe_square)  99.8 us
    another operation x16, other arithmetic, right_solve(): jax.scipy.linalg.solve_triangular(factor, jnp.swapaxes(values, 1, 2), low...  85.3 us
  transfers between devices with their start and end apart: 17, of which 17 were waited for; matrix products, arithmetic and copies ran while one was open for 2% of the time, Pallas kernels for 0%

commit v1 on v0

--- a/solution.py
+++ b/solution.py
@@ -9,7 +9,7 @@
 
 def spread(value, axis, source):
     kept = jnp.where(lax.axis_index(axis) == source, value, 0).astype(value.dtype)
-    return lax.psum(kept, axis)
+    return jnp.sum(lax.all_gather(kept, axis), axis=0)
 
 
 def lower_sym(square):

time: 1300 us -> 993 us (0.76)
  waiting for transfers between devices: 980 us -> 680 us
    psum x8 -> x0, waiting for transfers between devices: 641 us -> none  [spread(): return lax.psum(kept, axis)]
    all_gather x0 -> x8, waiting for transfers between devices: none -> 332 us  [spread(): return jnp.sum(lax.all_gather(kept, axis), axis=0)]
where the time goes in v1:
time: 993 us; the launch traced here: 984 us
  waiting for transfers between devices  680 us (68%)
  other arithmetic  203 us (20%)
  matrix products  40.2 us (4%)
  local copies, waits for them, and re-layouts  30 us (3%)
  between operations  15.5 us (2%)
    all_gather x8, waiting for transfers between devices, spread(): return jnp.sum(lax.all_gather(kept, axis), axis=0)  332 us
    all_gather x8, waiting for transfers between devices, local(): full_panel = lax.all_gather(my_panel, 'front', axis=1, tiled=True)  329 us
    another operation x24, other arithmetic, local(): own_factor = jnp.linalg.cholesky(safe_square)  99.6 us
    another operation x16, other arithmetic, right_solve(): jax.scipy.linalg.solve_triangular(factor, jnp.swapaxes(values, 1, 2), low...  80.7 us
  transfers between devices with their start and end apart: 17, of which 17 were waited for; matrix products, arithmetic and copies ran while one was open for 2% of the time, Pallas kernels for 0%

profile of v1, /device:TPU:0, one launch (start us, length us, event | category | flops | bytes accessed | tf_op | source)
XLA Modules:
  0.0 984.3 jit_solution(12024786861373492588)
XLA Ops:
  8.6 9.4 all_to_all.10
  18.1 3.6 all-to-all-start.1
  24.9 18.3 %all-to-all-done.1 = f32[1,8,3,128,128]{4,3,2,0,1:T(8,128)S(1)} async-done(((f32[1,8,3,128,128]{4,3,2,0,1:T(8,128)}), f32[1,8,3,128,128]{4,3,2,0,1:T(8,128)S(1)}, u32[]{:S(2)}, u32[]{:S(2)}) %all-to-all-start.1) | async-done | bytes 1572896 | tf_op jit(solution)/shard_map/all_to_all | solution.py:31
  43.2 2.6 fusion.31
  45.8 2.6 copy.467
  50.1 11.7 %custom-call.46 = f32[1,128,128]{2,1,0:T(8,128)S(1)} custom-call(f32[1,128,128]{2,1,0:T(8,128)S(1)} %copy.474), custom_call_target="Cholesky" | custom-call | tf_op jit(solution)/shard_map/jit(cholesky)/cholesky | solution.py:63
  63.9 43.5 %all-gather.41.cloned.1.call-done = f32[16,128,128]{2,1,0:T(8,128)} async-done(((f32[1,128,128]{2,1,0:T(8,128)}), f32[16,128,128]{2,1,0:T(8,128)}) %all-gather.41.cloned.1.call-update) | async-done | bytes 1048592 | tf_op jit(solution)/shard_map/all_gather | solution.py:12
  109.9 9.8 custom-call.47
  121.0 41.9 %all-gather.25.cloned.1.call-done = f32[1,2048,128]{2,1,0:T(8,128)} async-done(((f32[1,128,128]{2,1,0:T(8,128)}), f32[1,2048,128]{2,1,0:T(8,128)}) %all-gather.25.cloned.1.call-update) | async-done | bytes 1048592 | tf_op jit(solution)/shard_map/all_gather | solution.py:69
  162.9 2.2 fusion.13
  165.5 11.7 %custom-call.48 = f32[1,128,128]{2,1,0:T(8,128)S(1)} custom-call(f32[1,128,128]{2,1,0:T(8,128)S(1)} %copy.483), custom_call_target="Cholesky" | custom-call | tf_op jit(solution)/shard_map/jit(cholesky)/cholesky | solution.py:63
  179.3 42.2 %all-gather.43.cloned.1.call-done = f32[16,128,128]{2,1,0:T(8,128)} async-done(((f32[1,128,128]{2,1,0:T(8,128)}), f32[16,128,128]{2,1,0:T(8,128)}) %all-gather.43.cloned.1.call-update) | async-done | bytes 1048592 | tf_op jit(solution)/shard_map/all_gather | solution.py:12
  224.0 9.8 custom-call.49
  235.4 41.7 %all-gather.27.cloned.1.call-done = f32[1,2048,128]{2,1,0:T(8,128)} async-done(((f32[1,128,128]{2,1,0:T(8,128)}), f32[1,2048,128]{2,1,0:T(8,128)}) %all-gather.27.cloned.1.call-update) | async-done | bytes 1048592 | tf_op jit(solution)/shard_map/all_gather | solution.py:69
  277.1 2.1 fusion.12
  279.5 11.7 %custom-call.50 = f32[1,128,128]{2,1,0:T(8,128)S(1)} custom-call(f32[1,128,128]{2,1,0:T(8,128)S(1)} %copy.492), custom_call_target="Cholesky" | custom-call | tf_op jit(solution)/shard_map/jit(cholesky)/cholesky | solution.py:63
  293.3 42.2 %all-gather.45.cloned.1.call-done = f32[16,128,128]{2,1,0:T(8,128)} async-done(((f32[1,128,128]{2,1,0:T(8,128)}), f32[16,128,128]{2,1,0:T(8,128)}) %all-gather.45.cloned.1.call-update) | async-done | bytes 1048592 | tf_op jit(solution)/shard_map/all_gather | solution.py:12
  338.1 9.8 custom-call.51
  349.2 41.9 %all-gather.29.cloned.1.call-done = f32[1,2048,128]{2,1,0:T(8,128)} async-done(((f32[1,128,128]{2,1,0:T(8,128)}), f32[1,2048,128]{2,1,0:T(8,128)}) %all-gather.29.cloned.1.call-update) | async-done | bytes 1048592 | tf_op jit(solution)/shard_map/all_gather | solution.py:69
  391.1 2.0 fusion.11
  393.5 11.7 %custom-call.52 = f32[1,128,128]{2,1,0:T(8,128)S(1)} custom-call(f32[1,128,128]{2,1,0:T(8,128)S(1)} %fusion.97), custom_call_target="Cholesky" | custom-call | tf_op jit(solution)/shard_map/jit(cholesky)/cholesky | solution.py:63
  409.7 40.0 %all-gather.47.cloned.1.call-done = f32[16,128,128]{2,1,0:T(8,128)} async-done(((f32[1,128,128]{2,1,0:T(8,128)}), f32[16,128,128]{2,1,0:T(8,128)}) %all-gather.47.cloned.1.call-update) | async-done | bytes 1048592 | tf_op jit(solution)/shard_map/all_gather | solution.py:12
  452.5 9.8 custom-call.53
  463.9 42.2 %all-gather.31.cloned.1.call-done = f32[1,2048,128]{1,2,0:T(8,128)} async-done(((f32[1,128,128]{1,2,0:T(8,128)}), f32[1,2048,128]{1,2,0:T(8,128)}) %all-gather.31.cloned.1.call-update) | async-done | bytes 1048592 | tf_op jit(solution)/shard_map/all_gather | solution.py:69
  506.2 2.0 fusion.7
  508.5 11.7 %custom-call.54 = f32[1,128,128]{2,1,0:T(8,128)S(1)} custom-call(f32[1,128,128]{2,1,0:T(8,128)S(1)} %fusion.92), custom_call_target="Cholesky" | custom-call | tf_op jit(solution)/shard_map/jit(cholesky)/cholesky | solution.py:63
  522.5 42.2 %all-gather.49.cloned.1.call-done = f32[16,128,128]{2,1,0:T(8,128)} async-done(((f32[1,128,128]{2,1,0:T(8,128)}), f32[16,128,128]{2,1,0:T(8,128)}) %all-gather.49.cloned.1.call-update) | async-done | bytes 1048592 | tf_op jit(solution)/shard_map/all_gather | solution.py:12
  567.5 9.8 custom-call.55
  578.6 42.6 %all-gather.33.cloned.1.call-done = f32[1,2048,128]{1,2,0:T(8,128)} async-done(((f32[1,128,128]{1,2,0:T(8,128)}), f32[1,2048,128]{1,2,0:T(8,128)}) %all-gather.33.cloned.1.call-update) | async-done | bytes 1048592 | tf_op jit(solution)/shard_map/all_gather | solution.py:69
  621.2 1.9 fusion.5
  623.5 11.7 %custom-call.56 = f32[1,128,128]{2,1,0:T(8,128)S(1)} custom-call(f32[1,128,128]{2,1,0:T(8,128)S(1)} %fusion.87), custom_call_target="Cholesky" | custom-call | tf_op jit(solution)/shard_map/jit(cholesky)/cholesky | solution.py:63
  637.5 42.2 %all-gather.51.cloned.1.call-done = f32[16,128,128]{2,1,0:T(8,128)} async-done(((f32[1,128,128]{2,1,0:T(8,128)}), f32[16,128,128]{2,1,0:T(8,128)}) %all-gather.51.cloned.1.call-update) | async-done | bytes 1048592 | tf_op jit(solution)/shard_map/all_gather | solution.py:12
  682.5 9.8 custom-call.57
  693.8 42.4 %all-gather.35.cloned.1.call-done = f32[1,2048,128]{1,2,0:T(8,128)} async-done(((f32[1,128,128]{1,2,0:T(8,128)}), f32[1,2048,128]{1,2,0:T(8,128)}) %all-gather.35.cloned.1.call-update) | async-done | bytes 1048592 | tf_op jit(solution)/shard_map/all_gather | solution.py:69
  736.2 1.9 fusion.3
  738.4 11.7 %custom-call.58 = f32[1,128,128]{2,1,0:T(8,128)S(1)} custom-call(f32[1,128,128]{2,1,0:T(8,128)S(1)} %fusion.82), custom_call_target="Cholesky" | custom-call | tf_op jit(solution)/shard_map/jit(cholesky)/cholesky | solution.py:63
  752.4 42.2 %all-gather.53.cloned.1.call-done = f32[16,128,128]{2,1,0:T(8,128)} async-done(((f32[1,128,128]{2,1,0:T(8,128)}), f32[16,128,128]{2,1,0:T(8,128)}) %all-gather.53.cloned.1.call-update) | async-done | bytes 1048592 | tf_op jit(solution)/shard_map/all_gather | solution.py:12
  798.0 1.6 copy.535
  799.5 11.3 %custom-call.59 = f32[1,128,128]{1,2,0:T(8,128)} custom-call(f32[1,128,128]{2,1,0:T(8,128)} %copy.535), custom_call_target="InvertDiagBlocksLowerTriangular" | custom-call | tf_op jit(solution)/shard_map/jit(_solve_triangular)/triangular_solve | solution.py:20
  810.8 1.8 divide_dynamic-update-slice_fusion
  817.1 38.3 %all-gather.37.cloned.1.call-done = f32[1,2048,128]{1,2,0:T(8,128)} async-done(((f32[1,128,128]{1,2,0:T(8,128)}), f32[1,2048,128]{1,2,0:T(8,128)}) %all-gather.37.cloned.1.call-update) | async-done | bytes 1048592 | tf_op jit(solution)/shard_map/all_gather | solution.py:69
  855.5 2.2 fusion.1
  858.0 11.7 %custom-call.60 = f32[1,128,128]{2,1,0:T(8,128)S(1)} custom-call(f32[1,128,128]{2,1,0:T(8,128)S(1)} %fusion.77), custom_call_target="Cholesky" | custom-call | tf_op jit(solution)/shard_map/jit(cholesky)/cholesky | solution.py:63
  877.1 37.3 %all-gather.55.cloned.1.call-done = f32[16,128,128]{2,1,0:T(8,128)} async-done(((f32[1,128,128]{2,1,0:T(8,128)}), f32[16,128,128]{2,1,0:T(8,128)}) %all-gather.55.cloned.1.call-update) | async-done | bytes 1048592 | tf_op jit(solution)/shard_map/all_gather | solution.py:12
  915.8 9.8 custom-call.61
  932.0 38.2 %all-gather.39.cloned.1.call-done = f32[1,2048,128]{2,1,0:T(8,128)} async-done(((f32[1,128,128]{2,1,0:T(8,128)}), f32[1,2048,128]{2,1,0:T(8,128)}) %all-gather.39.cloned.1.call-update) | async-done | bytes 1048592 | tf_op jit(solution)/shard_map/all_gather | solution.py:69
  970.2 2.5 fusion.36
  972.7 1.7 select_select_fusion
  (259 shorter events, 75.9 us)
Async XLA Ops:
  18.1 25.1 %all-to-all-start.1 = ((f32[1,8,3,128,128]{4,3,2,0,1:T(8,128)}), f32[1,8,3,128,128]{4,3,2,0,1:T(8,128)S(1)}, u32[]{:S(2)}, u32[]{:S(2)}) async-start(f32[1,8,3,128,128]{4,3,2,0,1:T(8,128)} %bitcast.603), calls=%async_computation.1 | async-start | bytes 3145728 | tf_op jit(solution)/shard_map/all_to_all | solution.py:31
  21.7 85.7 %all-gather.41.cloned.1.call-start = ((), (), s32[]{:S(2)}) async-start(), calls=%async_computation.10 | async-start | bytes 1114112 | tf_op jit(solution)/shard_map/all_gather | solution.py:12
  63.8 99.1 %all-gather.25.cloned.1.call-start = ((), (), s32[]{:S(2)}) async-start(), calls=%async_computation.2 | async-start | bytes 1114112 | tf_op jit(solution)/shard_map/all_gather | solution.py:69
  120.7 100.8 %all-gather.43.cloned.1.call-start = ((), (), s32[]{:S(2)}) async-start(), calls=%async_computation.11 | async-start | bytes 1114112 | tf_op jit(solution)/shard_map/all_gather | solution.py:12
  179.2 97.8 %all-gather.27.cloned.1.call-start = ((), (), s32[]{:S(2)}) async-start(), calls=%async_computation.3 | async-start | bytes 1114112 | tf_op jit(solution)/shard_map/all_gather | solution.py:69
  234.8 100.7 %all-gather.45.cloned.1.call-start = ((), (), s32[]{:S(2)}) async-start(), calls=%async_computation.12 | async-start | bytes 1114112 | tf_op jit(solution)/shard_map/all_gather | solution.py:12
  293.2 97.9 %all-gather.29.cloned.1.call-start = ((), (), s32[]{:S(2)}) async-start(), calls=%async_computation.4 | async-start | bytes 1114112 | tf_op jit(solution)/shard_map/all_gather | solution.py:69
  347.9 1.3 copy-start.12
  348.8 100.9 %all-gather.47.cloned.1.call-start = ((), (), s32[]{:S(2)}) async-start(), calls=%async_computation.13 | async-start | bytes 1114112 | tf_op jit(solution)/shard_map/all_gather | solution.py:12
  407.5 98.7 %all-gather.31.cloned.1.call-start = ((), (), s32[]{:S(2)}) async-start(), calls=%async_computation.5 | async-start | bytes 1114112 | tf_op jit(solution)/shard_map/all_gather | solution.py:69
  462.3 1.3 copy-start.14
  463.3 101.5 %all-gather.49.cloned.1.call-start = ((), (), s32[]{:S(2)}) async-start(), calls=%async_computation.14 | async-start | bytes 1114112 | tf_op jit(solution)/shard_map/all_gather | solution.py:12
  463.6 42.6 %copy-start.10 = (f32[1,128,128]{1,2,0:T(8,128)S(1)}, f32[1,128,128]{1,2,0:T(8,128)}, u32[]{:S(2)}) copy-start(f32[1,128,128]{1,2,0:T(8,128)} %get-tuple-element.376) | copy-start | bytes 196612
  522.5 98.7 %all-gather.33.cloned.1.call-start = ((), (), s32[]{:S(2)}) async-start(), calls=%async_computation.6 | async-start | bytes 1114112 | tf_op jit(solution)/shard_map/all_gather | solution.py:69
  577.3 1.3 copy-start.16
  578.3 101.4 %all-gather.51.cloned.1.call-start = ((), (), s32[]{:S(2)}) async-start(), calls=%async_computation.15 | async-start | bytes 1114112 | tf_op jit(solution)/shard_map/all_gather | solution.py:12
  637.5 98.7 %all-gather.35.cloned.1.call-start = ((), (), s32[]{:S(2)}) async-start(), calls=%async_computation.7 | async-start | bytes 1114112 | tf_op jit(solution)/shard_map/all_gather | solution.py:69
  692.3 45.7 %copy-start.18 = (f32[1,128,128]{1,2,0:T(8,128)}, f32[1,128,128]{1,2,0:T(8,128)S(1)}, u32[]{:S(2)}) copy-start(f32[1,128,128]{1,2,0:T(8,128)S(1)} %custom-call.57) | copy-start | bytes 196612
  693.3 101.4 %all-gather.53.cloned.1.call-start = ((), (), s32[]{:S(2)}) async-start(), calls=%async_computation.16 | async-start | bytes 1114112 | tf_op jit(solution)/shard_map/all_gather | solution.py:12
  738.4 74.5 %copy-start.11 = (f32[1,64,2048]{2,1,0:T(8,128)S(1)}, f32[1,64,2048]{2,1,0:T(8,128)}, u32[]{:S(2)}) copy-start(f32[1,64,2048]{2,1,0:T(8,128)} %param.78) | copy-start | bytes 1572868
  750.2 63.5 %copy-start = (f32[1,2048,128]{2,1,0:T(8,128)S(1)}, f32[1,2048,128]{2,1,0:T(8,128)}, u32[]{:S(2)}) copy-start(f32[1,2048,128]{2,1,0:T(8,128)} %all-gather.25.cloned.1.call-done) | copy-start | bytes 3145732
  752.4 103.1 %all-gather.37.cloned.1.call-start = ((), (), s32[]{:S(2)}) async-start(), calls=%async_computation.8 | async-start | bytes 1114112 | tf_op jit(solution)/shard_map/all_gather | solution.py:69
  797.3 18.4 %copy-start.1 = (f32[1,2048,128]{2,1,0:T(8,128)S(1)}, f32[1,2048,128]{2,1,0:T(8,128)}, u32[]{:S(2)}) copy-start(f32[1,2048,128]{2,1,0:T(8,128)} %all-gather.27.cloned.1.call-done) | copy-start | bytes 3145732
  812.6 101.8 %all-gather.55.cloned.1.call-start = ((), (), s32[]{:S(2)}) async-start(), calls=%async_computation.17 | async-start | bytes 1114112 | tf_op jit(solution)/shard_map/all_gather | solution.py:12
  816.8 38.6 %copy-start.9 = (f32[1,128,128]{1,2,0:T(8,128)S(1)}, f32[1,128,128]{1,2,0:T(8,128)}, u32[]{:S(2)}) copy-start(f32[1,128,128]{1,2,0:T(8,128)} %get-tuple-element.382) | copy-start | bytes 196612
  817.1 55.3 %copy-start.13 = (f32[1,128,128]{1,2,0:T(8,128)S(1)}, f32[1,128,128]{1,2,0:T(8,128)}, u32[]{:S(2)}) copy-start(f32[1,128,128]{1,2,0:T(8,128)} %copy-done.12) | copy-start | bytes 196612
  817.1 56.1 %copy-start.2 = (f32[1,2048,128]{2,1,0:T(8,128)S(1)}, f32[1,2048,128]{2,1,0:T(8,128)}, u32[]{:S(2)}) copy-start(f32[1,2048,128]{2,1,0:T(8,128)} %all-gather.29.cloned.1.call-done) | copy-start | bytes 3145732
  857.7 16.6 %copy-start.15 = (f32[1,128,128]{1,2,0:T(8,128)S(1)}, f32[1,128,128]{1,2,0:T(8,128)}, u32[]{:S(2)}) copy-start(f32[1,128,128]{1,2,0:T(8,128)} %copy-done.14) | copy-start | bytes 196612
  857.8 17.4 %copy-start.3 = (f32[1,2048,128]{1,2,0:T(8,128)S(1)}, f32[1,2048,128]{1,2,0:T(8,128)}, u32[]{:S(2)}) copy-start(f32[1,2048,128]{1,2,0:T(8,128)} %all-gather.31.cloned.1.call-done) | copy-start | bytes 3145732
  872.1 98.1 %all-gather.39.cloned.1.call-start = ((), (), s32[]{:S(2)}) async-start(), calls=%async_computation.9 | async-start | bytes 1114112 | tf_op jit(solution)/shard_map/all_gather | solution.py:69
  873.2 2.5 copy-start.17
  873.2 3.3 copy-start.4
  876.5 51.4 %copy-start.19 = (f32[1,128,128]{1,2,0:T(8,128)S(1)}, f32[1,128,128]{1,2,0:T(8,128)}, u32[]{:S(2)}) copy-start(f32[1,128,128]{1,2,0:T(8,128)} %copy-done.18) | copy-start | bytes 196612
  877.1 51.6 %copy-start.5 = (f32[1,2048,128]{1,2,0:T(8,128)S(1)}, f32[1,2048,128]{1,2,0:T(8,128)}, u32[]{:S(2)}) copy-start(f32[1,2048,128]{1,2,0:T(8,128)} %all-gather.35.cloned.1.call-done) | copy-start | bytes 3145732
  915.7 13.5 %copy-start.20 = (f32[1,128,128]{1,2,0:T(8,128)S(1)}, f32[1,128,128]{1,2,0:T(8,128)}, u32[]{:S(2)}) copy-start(f32[1,128,128]{1,2,0:T(8,128)} %custom-call.59) | copy-start | bytes 196612
  915.7 14.3 %copy-start.6 = (f32[1,2048,128]{1,2,0:T(8,128)S(1)}, f32[1,2048,128]{1,2,0:T(8,128)}, u32[]{:S(2)}) copy-start(f32[1,2048,128]{1,2,0:T(8,128)} %all-gather.37.cloned.1.call-done) | copy-start | bytes 3145732
  928.7 41.5 %copy-start.8 = (f32[1,128,128]{2,1,0:T(8,128)S(1)}, f32[1,128,128]{2,1,0:T(8,128)}, u32[]{:S(2)}) copy-start(f32[1,128,128]{2,1,0:T(8,128)} %get-tuple-element.384) | copy-start | bytes 196612
  974.4 1.3 copy-start.7
  974.4 1.6 copy-start.21
  976.7 0.8 copy-start.22
Sparse Core Ops, SparseCore 0:
  63.9 43.3 all-gather.40
  120.8 42.0 all-gather.24
  179.3 42.0 all-gather.42
  234.9 42.0 all-gather.26
  293.4 42.0 all-gather.44
  349.0 42.0 all-gather.28
  407.6 42.1 all-gather.46
  463.4 42.7 all-gather.30
  522.6 42.1 all-gather.48
  578.5 42.7 all-gather.32
  637.6 42.1 all-gather.50
  693.4 42.7 all-gather.34
  752.5 42.1 all-gather.52
  812.7 42.7 all-gather.36
  872.3 42.1 all-gather.54
  928.0 42.1 all-gather.38
